TPU v7x, 32 devices: a whole 2x2x4 slice. The times are simulated.
32 devices in a mesh: space: 16 (over z, y, x), mem: 2 (over core).
Axes of the slice: x: 2, y: 2, z: 4, core: 2. Of those that a mesh axis runs over, the one named last changes fastest.
Arguments:
- perturb: float32 [1024, 4096], P(('space', 'mem')), may hold values from -6 to 6
- pair_list: int32 [64, 3], P('space'), may hold values from 0 to 15, as said below
- pair_count: int32 [16], P('space'), may hold values from 1 to 4, as said below
- band_weight: float32 [8], replicated, may hold values from 0.25 to 1
- cov_scale: float32 [1], replicated, may hold values from 0.5 to 2
- target: float32 [4096, 1024], P('space', 'mem'), may hold values from -6 to 6
- first_guess: float32 [4096, 1024], P('space', 'mem'), may hold values from -6 to 6
Outputs:
- solution: float32 [4096, 1024], P('space', 'mem')
Inputs may be any that keep to these rules, and one draw needn't show every extreme that they name: `pair_list`: rows 4 * s to 4 * s + 3 are owner s's slots. The first block of each is owner s's own block s; the second is the first plus d modulo 16, with 0 <= d <= 3; each of the four pairs (d = 0 to 3) stands in exactly one slot of its owner. The third column is an index into band_weight. Only the first pair_count[s] slots of owner s are live; in every draw some owner has all 4 slots live.
All inputs are finite; a program needn't handle non-finite values.
Results may differ from a plain program's by a relative error of at most 0.0003.
Values sent between devices are 32-bit elements; how exact they have to be, the bound alone decides.
A program may use at most 64 MiB of HBM per device.

v0:
```python
import jax
import jax.numpy as jnp
from jax import lax
from jax.sharding import PartitionSpec as P

BLOCK = 256
MEMBERS = 1024
REACH_DEV = 3
NBANDS = 8
ITERS = 2


def shifted(array, axis, by):
    count = lax.axis_size(axis)
    return lax.ppermute(array, axis, [(i, (i + by) % count) for i in range(count)])


def mm(a, b, ca, cb):
    return lax.dot_general(
        a,
        b,
        (((ca,), (cb,)), ((), ())),
        precision=lax.Precision.HIGH,
        preferred_element_type=jnp.float32,
    )


def gap_weights(pair_list, pair_count, band_weight, cov_scale):
    slots = pair_list.shape[0]
    blocks_all = lax.axis_size("space")
    gap = (pair_list[:, 1] - pair_list[:, 0]) % blocks_all
    living = (jnp.arange(slots, dtype=jnp.int32) < pair_count[0]).astype(jnp.float32)
    bands = jnp.arange(NBANDS, dtype=jnp.int32)
    band_now = jnp.sum(
        jnp.where(pair_list[:, 2][:, None] == bands[None, :], band_weight[None, :], 0.0), axis=1
    )
    slot_weight = cov_scale[0] * band_now * living / (MEMBERS - 1)
    gaps = jnp.arange(REACH_DEV + 1, dtype=jnp.int32)
    return jnp.sum(jnp.where(gap[:, None] == gaps[None, :], slot_weight[:, None], 0.0), axis=0)


def per_device(perturb, pair_list, pair_count, band_weight, cov_scale, target, first_guess):
    w = gap_weights(pair_list, pair_count, band_weight, cov_scale)
    w_next = shifted(w, "space", -1)
    p0 = lax.all_to_all(perturb, "space", split_axis=1, concat_axis=0, tiled=True)
    p1 = shifted(p0, "space", -1)
    p3 = shifted(p0, "space", -3)
    x0 = first_guess
    t0 = mm(p0, p0, 0, 0) * w[0]
    t1 = mm(p0, p1, 0, 0) * w[1]
    t3 = mm(p0, p3, 0, 0) * w[3]
    t2 = mm(p1, p3, 0, 0) * w_next[2]
    t0, t1, t2, t3 = lax.psum((t0, t1, t2, t3), "mem")
    for sweep in range(ITERS):
        x1 = shifted(x0, "space", -1)
        x3 = shifted(x0, "space", -3)
        back1 = shifted(mm(t1, x0, 0, 0) + mm(t2, x3, 1, 0), "space", 1)
        back3 = shifted(mm(t3, x0, 0, 0) + mm(t2, x1, 0, 0), "space", 3)
        own = mm(t0, x0, 1, 0) + mm(t1, x1, 1, 0) + mm(t3, x3, 1, 0)
        x0 = x0 + 0.5 * (target - x0 - (own + back1 + back3))
    return x0


def solution(mesh):
    in_specs = (
        P(("space", "mem"), None),
        P("space", None),
        P("space"),
        P(),
        P(),
        P("space", "mem"),
        P("space", "mem"),
    )
    out_specs = P("space", "mem")
    return jax.shard_map(
        per_device, mesh=mesh, in_specs=in_specs, out_specs=out_specs, check_vma=False
    )
```

profile of v0, /device:TPU:2, one launch (start us, length us, event | category | flops | bytes accessed | tf_op | source)
XLA Modules:
  0.0 171.7 jit_solution(16885605686824143802)
XLA Ops:
  6.5 1.9 %copy.12 = f32[4,16,8,256]{3,2,0,1:T(8,128)} copy(f32[4,16,8,256]{3,2,1,0:T(8,128)} %bitcast.59) | data formatting | bytes 1048576 | tf_op jit(solution)/shard_map/all_to_all | solution.py:45
  8.4 7.3 %all-to-all-start = ((f32[32,16,256]{2,0,1:T(8,128)}), f32[32,16,256]{2,0,1:T(8,128)S(1)}, u32[]{:S(2)}, u32[]{:S(2)}) async-start(f32[32,16,256]{2,0,1:T(8,128)} %bitcast.52), calls=%async_computation | async-start | bytes 1048576 | tf_op jit(solution)/shard_map/all_to_all | solution.py:45
  17.3 0.7 copy-done.7
  18.2 11.3 %all-to-all-done = f32[32,16,256]{2,0,1:T(8,128)S(1)} async-done(((f32[32,16,256]{2,0,1:T(8,128)}), f32[32,16,256]{2,0,1:T(8,128)S(1)}, u32[]{:S(2)}, u32[]{:S(2)}) %all-to-all-start) | async-done | bytes 524320 | tf_op jit(solution)/shard_map/all_to_all | solution.py:45
  29.5 1.5 collective-permute-start
  31.0 2.6 %collective-permute-start.4 = (f32[4]{0:T(128)S(1)}, f32[4]{0:T(128)S(1)}, u32[]{:S(2)}, u32[]{:S(2)}) collective-permute-start(f32[4]{0:T(128)S(1)} %select_reduce_fusion), channel_id=1, source_target_pairs={{0,30},{2,0},{4,2},{6,4},{8,6},{10,8},{12,10},{14,12},{16,14},{18,... | collective-permute-start | bytes 56 | tf_op jit(solution)/shard_map/ppermute | solution.py:15
  33.6 1.4 collective-permute-start.2
  35.0 0.6 fusion.12
  35.6 17.6 %collective-permute-done.4 = f32[4]{0:T(128)S(1)} collective-permute-done((f32[4]{0:T(128)S(1)}, f32[4]{0:T(128)S(1)}, u32[]{:S(2)}, u32[]{:S(2)}) %collective-permute-start.4) | collective-permute-done | bytes 48 | tf_op jit(solution)/shard_map/ppermute | solution.py:15
  53.2 0.6 slice.27
  53.8 1.9 %fusion.7 = f32[256,256]{1,0:T(8,128)} fusion(f32[32,16,256]{2,0,1:T(8,128)S(1)} %all-to-all-done, f32[]{:T(128)} %bitcast.4), kind=kOutput, calls=%fused_computation.16 | convolution fusion | flops 201392128 | bytes 786436 | tf_op jit(solution)/shard_map/dot_general | solution.py:19
  55.7 1.9 %convolution_multiply_fusion.2 = f32[256,256]{1,0:T(8,128)} fusion(f32[512,256]{1,0:T(8,128)S(1)} %bitcast.57, f32[512,256]{1,0:T(8,128)S(1)} %collective-permute-done, f32[]{:T(128)} %bitcast.7), kind=kOutput, calls=%fused_computation.19 | convolution fusion | flops 201392128 | bytes 1310724 | tf_op jit(solution)/shard_map/dot_general | solution.py:19
  57.6 2.0 %convolution_multiply_fusion.1 = f32[256,256]{1,0:T(8,128)} fusion(f32[512,256]{1,0:T(8,128)S(1)} %bitcast.58, f32[512,256]{1,0:T(8,128)S(1)} %collective-permute-done.2, f32[]{:T(128)} %bitcast.8), kind=kOutput, calls=%fused_computation.18 | convolution fusion | flops 201392128 | bytes 1310724 | tf_op jit(solution)/shard_map/dot_general | solution.py:19
  59.6 1.9 %convolution_multiply_fusion = f32[256,256]{1,0:T(8,128)} fusion(f32[512,256]{1,0:T(8,128)S(1)} %collective-permute-done, f32[512,256]{1,0:T(8,128)S(1)} %collective-permute-done.2, f32[]{:T(128)} %bitcast.9), kind=kOutput, calls=%fused_computation.17 | convolution fusion | flops 201392128 | bytes 1310724 | tf_op jit(solution)/shard_map/dot_general | solution.py:19
  61.5 1.0 copy-done
  62.5 1.8 %collective-permute-start.3 = (f32[256,512]{1,0:T(8,128)S(1)}, f32[256,512]{1,0:T(8,128)S(1)}, u32[]{:S(2)}, u32[]{:S(2)}) collective-permute-start(f32[256,512]{1,0:T(8,128)S(1)} %copy-done), channel_id=1, source_target_pairs={{0,26},{2,28},{4,30},{6,0},{8,2},{10,4},{12,6},{14,8},{16,10},{18,... | collective-permute-start | bytes 1572872 | tf_op jit(solution)/shard_map/ppermute | solution.py:15
  64.2 2.5 %collective-permute-start.1 = (f32[256,512]{1,0:T(8,128)S(1)}, f32[256,512]{1,0:T(8,128)S(1)}, u32[]{:S(2)}, u32[]{:S(2)}) collective-permute-start(f32[256,512]{1,0:T(8,128)S(1)} %copy-done), channel_id=1, source_target_pairs={{0,30},{2,0},{4,2},{6,4},{8,6},{10,8},{12,10},{14,12},{16,14},{18,... | collective-permute-start | bytes 1572872 | tf_op jit(solution)/shard_map/ppermute | solution.py:15
  66.8 14.8 %all-reduce.3.cloned.1.call-done = (f32[256,256]{1,0:T(8,128)}, f32[256,256]{1,0:T(8,128)}, f32[256,256]{1,0:T(8,128)}, f32[256,256]{1,0:T(8,128)}) async-done(((f32[256,256]{1,0:T(8,128)}, f32[256,256]{1,0:T(8,128)}, f32[256,256]{1,0:T(8,128)}, f32[256,256]{1,0:T(8,128)}), (f32[256,256]{1,0:T(8,128)}, f32[256,256]{1,0:T(8,128)}, f32[256,256]{1,0:T(8,128)}, ...) | async-done | bytes 1048592 | tf_op jit(solution)/shard_map/psum | solution.py:53
  81.6 1.4 fusion.14
  83.4 1.5 collective-permute-start.5
  85.8 2.0 %collective-permute-start.6 = (f32[256,512]{1,0:T(8,128)S(1)}, f32[256,512]{1,0:T(8,128)S(1)}, u32[]{:S(2)}, u32[]{:S(2)}) collective-permute-start(f32[256,512]{1,0:T(8,128)S(1)} %convolution_add_fusion.4), channel_id=1, source_target_pairs={{0,6},{2,8},{4,10},{6,12},{8,14},{10,16},{12,18},{14,20},{16,22},{... | collective-permute-start | bytes 1572872 | tf_op jit(solution)/shard_map/ppermute | solution.py:15
  88.2 0.6 copy-done.1
  89.2 18.7 %collective-permute-done.5 = f32[256,512]{1,0:T(8,128)S(1)} collective-permute-done((f32[256,512]{1,0:T(8,128)S(1)}, f32[256,512]{1,0:T(8,128)S(1)}, u32[]{:S(2)}, u32[]{:S(2)}) %collective-permute-start.5) | collective-permute-done | bytes 524320 | tf_op jit(solution)/shard_map/ppermute | solution.py:15
  107.8 0.5 fusion.6
  108.3 6.2 %collective-permute-start.8 = (f32[256,512]{1,0:T(8,128)S(1)}, f32[256,512]{1,0:T(8,128)S(1)}, u32[]{:S(2)}, u32[]{:S(2)}) collective-permute-start(f32[256,512]{1,0:T(8,128)S(1)} %fusion.6), channel_id=1, source_target_pairs={{0,26},{2,28},{4,30},{6,0},{8,2},{10,4},{12,6},{14,8},{16,10},{18,... | collective-permute-start | bytes 1572872 | tf_op jit(solution)/shard_map/ppermute | solution.py:15
  114.5 10.8 %collective-permute-done.8 = f32[256,512]{1,0:T(8,128)S(1)} collective-permute-done((f32[256,512]{1,0:T(8,128)S(1)}, f32[256,512]{1,0:T(8,128)S(1)}, u32[]{:S(2)}, u32[]{:S(2)}) %collective-permute-start.8) | collective-permute-done | bytes 524320 | tf_op jit(solution)/shard_map/ppermute | solution.py:15
  126.1 3.4 %collective-permute-start.9 = (f32[256,512]{1,0:T(8,128)S(1)}, f32[256,512]{1,0:T(8,128)S(1)}, u32[]{:S(2)}, u32[]{:S(2)}) collective-permute-start(f32[256,512]{1,0:T(8,128)S(1)} %convolution_add_fusion.1), channel_id=1, source_target_pairs={{0,2},{2,4},{4,6},{6,8},{8,10},{10,12},{12,14},{14,16},{16,18},{18... | collective-permute-start | bytes 1572872 | tf_op jit(solution)/shard_map/ppermute | solution.py:15
  129.5 7.0 %collective-permute-done.7 = f32[256,512]{1,0:T(8,128)S(1)} collective-permute-done((f32[256,512]{1,0:T(8,128)S(1)}, f32[256,512]{1,0:T(8,128)S(1)}, u32[]{:S(2)}, u32[]{:S(2)}) %collective-permute-start.7) | collective-permute-done | bytes 524320 | tf_op jit(solution)/shard_map/ppermute | solution.py:15
  137.3 1.7 %collective-permute-start.10 = (f32[256,512]{1,0:T(8,128)S(1)}, f32[256,512]{1,0:T(8,128)S(1)}, u32[]{:S(2)}, u32[]{:S(2)}) collective-permute-start(f32[256,512]{1,0:T(8,128)S(1)} %convolution_add_fusion), channel_id=1, source_target_pairs={{0,6},{2,8},{4,10},{6,12},{8,14},{10,16},{12,18},{14,20},{16,22},{... | collective-permute-start | bytes 1572872 | tf_op jit(solution)/shard_map/ppermute | solution.py:15
  139.9 18.9 %collective-permute-done.9 = f32[256,512]{1,0:T(8,128)S(1)} collective-permute-done((f32[256,512]{1,0:T(8,128)S(1)}, f32[256,512]{1,0:T(8,128)S(1)}, u32[]{:S(2)}, u32[]{:S(2)}) %collective-permute-start.9) | collective-permute-done | bytes 524320 | tf_op jit(solution)/shard_map/ppermute | solution.py:15
  158.8 4.7 %collective-permute-done.10 = f32[256,512]{1,0:T(8,128)S(1)} collective-permute-done((f32[256,512]{1,0:T(8,128)S(1)}, f32[256,512]{1,0:T(8,128)S(1)}, u32[]{:S(2)}, u32[]{:S(2)}) %collective-permute-start.10) | collective-permute-done | bytes 524320 | tf_op jit(solution)/shard_map/ppermute | solution.py:15
  163.6 1.3 multiply_add_fusion
  (36 shorter events, 5.0 us)
Async XLA Ops:
  8.4 21.0 %all-to-all-start = ((f32[32,16,256]{2,0,1:T(8,128)}), f32[32,16,256]{2,0,1:T(8,128)S(1)}, u32[]{:S(2)}, u32[]{:S(2)}) async-start(f32[32,16,256]{2,0,1:T(8,128)} %bitcast.52), calls=%async_computation | async-start | bytes 1048576 | tf_op jit(solution)/shard_map/all_to_all | solution.py:45
  15.7 1.4 copy-start.6
  15.7 65.8 %all-reduce.3.cloned.1.call-start = ((), (), s32[]{:S(2)}) async-start(), calls=%async_computation.1 | async-start | bytes 2097152 | tf_op jit(solution)/shard_map/psum | solution.py:53
  17.3 0.7 copy-start.7
  29.5 26.3 %collective-permute-start = (f32[512,256]{1,0:T(8,128)S(1)}, f32[512,256]{1,0:T(8,128)S(1)}, u32[]{:S(2)}, u32[]{:S(2)}) collective-permute-start(f32[512,256]{1,0:T(8,128)S(1)} %bitcast.55), channel_id=1, source_target_pairs={{0,30},{2,0},{4,2},{6,4},{8,6},{10,8},{12,10},{14,12},{16,14},{18,... | collective-permute-start | bytes 1572872 | tf_op jit(solution)/shard_map/ppermute | solution.py:15
  31.0 22.2 %collective-permute-start.4 = (f32[4]{0:T(128)S(1)}, f32[4]{0:T(128)S(1)}, u32[]{:S(2)}, u32[]{:S(2)}) collective-permute-start(f32[4]{0:T(128)S(1)} %select_reduce_fusion), channel_id=1, source_target_pairs={{0,30},{2,0},{4,2},{6,4},{8,6},{10,8},{12,10},{14,12},{16,14},{18,... | collective-permute-start | bytes 56 | tf_op jit(solution)/shard_map/ppermute | solution.py:15
  33.6 24.0 %collective-permute-start.2 = (f32[512,256]{1,0:T(8,128)S(1)}, f32[512,256]{1,0:T(8,128)S(1)}, u32[]{:S(2)}, u32[]{:S(2)}) collective-permute-start(f32[512,256]{1,0:T(8,128)S(1)} %bitcast.56), channel_id=1, source_target_pairs={{0,26},{2,28},{4,30},{6,0},{8,2},{10,4},{12,6},{14,8},{16,10},{18,... | collective-permute-start | bytes 1572872 | tf_op jit(solution)/shard_map/ppermute | solution.py:15
  61.4 1.0 copy-start
  62.5 20.5 %collective-permute-start.3 = (f32[256,512]{1,0:T(8,128)S(1)}, f32[256,512]{1,0:T(8,128)S(1)}, u32[]{:S(2)}, u32[]{:S(2)}) collective-permute-start(f32[256,512]{1,0:T(8,128)S(1)} %copy-done), channel_id=1, source_target_pairs={{0,26},{2,28},{4,30},{6,0},{8,2},{10,4},{12,6},{14,8},{16,10},{18,... | collective-permute-start | bytes 1572872 | tf_op jit(solution)/shard_map/ppermute | solution.py:15
  64.2 21.1 %collective-permute-start.1 = (f32[256,512]{1,0:T(8,128)S(1)}, f32[256,512]{1,0:T(8,128)S(1)}, u32[]{:S(2)}, u32[]{:S(2)}) collective-permute-start(f32[256,512]{1,0:T(8,128)S(1)} %copy-done), channel_id=1, source_target_pairs={{0,30},{2,0},{4,2},{6,4},{8,6},{10,8},{12,10},{14,12},{16,14},{18,... | collective-permute-start | bytes 1572872 | tf_op jit(solution)/shard_map/ppermute | solution.py:15
  81.6 1.4 copy-start.2
  83.0 1.9 %copy-start.3 = (f32[256,256]{1,0:T(8,128)S(1)}, f32[256,256]{1,0:T(8,128)}, u32[]{:S(2)}) copy-start(f32[256,256]{1,0:T(8,128)} %get-tuple-element.7) | copy-start | bytes 786436
  83.4 24.4 %collective-permute-start.5 = (f32[256,512]{1,0:T(8,128)S(1)}, f32[256,512]{1,0:T(8,128)S(1)}, u32[]{:S(2)}, u32[]{:S(2)}) collective-permute-start(f32[256,512]{1,0:T(8,128)S(1)} %convolution_add_fusion.5), channel_id=1, source_target_pairs={{0,2},{2,4},{4,6},{6,8},{8,10},{10,12},{12,14},{14,16},{16,18},{18... | collective-permute-start | bytes 1572872 | tf_op jit(solution)/shard_map/ppermute | solution.py:15
  85.4 2.4 %copy-start.5 = (f32[256,256]{1,0:T(8,128)S(1)}, f32[256,256]{1,0:T(8,128)}, u32[]{:S(2)}) copy-start(f32[256,256]{1,0:T(8,128)} %get-tuple-element.10) | copy-start | bytes 786436
  85.8 22.0 %collective-permute-start.6 = (f32[256,512]{1,0:T(8,128)S(1)}, f32[256,512]{1,0:T(8,128)S(1)}, u32[]{:S(2)}, u32[]{:S(2)}) collective-permute-start(f32[256,512]{1,0:T(8,128)S(1)} %convolution_add_fusion.4), channel_id=1, source_target_pairs={{0,6},{2,8},{4,10},{6,12},{8,14},{10,16},{12,18},{14,20},{16,22},{... | collective-permute-start | bytes 1572872 | tf_op jit(solution)/shard_map/ppermute | solution.py:15
  87.8 1.0 copy-start.1
  88.7 19.1 %copy-start.4 = (f32[256,512]{1,0:T(8,128)S(1)}, f32[256,512]{1,0:T(8,128)}, u32[]{:S(2)}) copy-start(f32[256,512]{1,0:T(8,128)} %param.12) | copy-start | bytes 1572868
  108.3 17.0 %collective-permute-start.8 = (f32[256,512]{1,0:T(8,128)S(1)}, f32[256,512]{1,0:T(8,128)S(1)}, u32[]{:S(2)}, u32[]{:S(2)}) collective-permute-start(f32[256,512]{1,0:T(8,128)S(1)} %fusion.6), channel_id=1, source_target_pairs={{0,26},{2,28},{4,30},{6,0},{8,2},{10,4},{12,6},{14,8},{16,10},{18,... | collective-permute-start | bytes 1572872 | tf_op jit(solution)/shard_map/ppermute | solution.py:15
  114.5 21.9 %collective-permute-start.7 = (f32[256,512]{1,0:T(8,128)S(1)}, f32[256,512]{1,0:T(8,128)S(1)}, u32[]{:S(2)}, u32[]{:S(2)}) collective-permute-start(f32[256,512]{1,0:T(8,128)S(1)} %fusion.6), channel_id=1, source_target_pairs={{0,30},{2,0},{4,2},{6,4},{8,6},{10,8},{12,10},{14,12},{16,14},{18,... | collective-permute-start | bytes 1572872 | tf_op jit(solution)/shard_map/ppermute | solution.py:15
  126.1 32.7 %collective-permute-start.9 = (f32[256,512]{1,0:T(8,128)S(1)}, f32[256,512]{1,0:T(8,128)S(1)}, u32[]{:S(2)}, u32[]{:S(2)}) collective-permute-start(f32[256,512]{1,0:T(8,128)S(1)} %convolution_add_fusion.1), channel_id=1, source_target_pairs={{0,2},{2,4},{4,6},{6,8},{8,10},{10,12},{12,14},{14,16},{16,18},{18... | collective-permute-start | bytes 1572872 | tf_op jit(solution)/shard_map/ppermute | solution.py:15
  137.3 26.2 %collective-permute-start.10 = (f32[256,512]{1,0:T(8,128)S(1)}, f32[256,512]{1,0:T(8,128)S(1)}, u32[]{:S(2)}, u32[]{:S(2)}) collective-permute-start(f32[256,512]{1,0:T(8,128)S(1)} %convolution_add_fusion), channel_id=1, source_target_pairs={{0,6},{2,8},{4,10},{6,12},{8,14},{10,16},{12,18},{14,20},{16,22},{... | collective-permute-start | bytes 1572872 | tf_op jit(solution)/shard_map/ppermute | solution.py:15
Sparse Core Ops, SparseCore 0:
  61.6 19.9 all-reduce.2
where the time goes:
time: 172 us
  waiting for transfers between devices  104 us (60%)
  starting transfers between devices  31.9 us (19%)
  matrix products  15.3 us (9%)
  between operations  14.9 us (9%)
  local copies, waits for them, and re-layouts  5.37 us (3%)
    ppermute x11, waiting for transfers between devices, shifted(): lax.ppermute(array, axis, [(i, (i + by) % count) for i in range(count)])  77.7 us
    ppermute x11, starting transfers between devices, shifted(): lax.ppermute(array, axis, [(i, (i + by) % count) for i in range(count)])  24.6 us
    dot_general x18, matrix products, mm(): lax.dot_general(a, b, (((ca,), (cb,)), ((), ())), precision=lax.Precision...  15.3 us
    psum x1, waiting for transfers between devices, per_device(): t0, t1, t2, t3 = lax.psum((t0, t1, t2, t3), 'mem')  14.8 us
    all_to_all x1, waiting for transfers between devices, per_device(): lax.all_to_all(perturb, 'space', split_axis=1, concat_axis=0, tiled=True)  11.3 us
    all_to_all x1, starting transfers between devices, per_device(): lax.all_to_all(perturb, 'space', split_axis=1, concat_axis=0, tiled=True)  7.31 us
  transfers between devices with their start and end apart: 13, of which 8 were waited for; matrix products, arithmetic and copies ran while one was open for 7% of the time, Pallas kernels for 0%

commit v1 on v0

--- a/solution.py
+++ b/solution.py
@@ -8,6 +8,29 @@
 REACH_DEV = 3
 NBANDS = 8
 ITERS = 2
+
+
+def split_up(x, dim, count):
+    before, after = (x.shape[:dim], x.shape[dim + 1 :])
+    return jnp.moveaxis(x.reshape(*before, count, -1, *after), dim, 0)
+
+
+def in_order(blocks, dim):
+    lengths = list(blocks.shape[1:])
+    lengths[dim] *= blocks.shape[0]
+    return jnp.moveaxis(blocks, 0, dim).reshape(lengths)
+
+
+def rotated_exchange(x, axis, split_dim, concat_dim):
+    length, index = (lax.axis_size(axis), lax.axis_index(axis))
+    parts = split_up(x, split_dim, length)
+    out = parts
+    for lap in range(1, length):
+        target, source = ((index + lap) % length, (index - lap) % length)
+        sent = lax.dynamic_index_in_dim(parts, target, 0)
+        other = lax.ppermute(sent, axis, [(i, (i + lap) % length) for i in range(length)])
+        out = lax.dynamic_update_slice_in_dim(out, other, source, axis=0)
+    return in_order(out, concat_dim)
 
 
 def shifted(array, axis, by):
@@ -42,7 +65,7 @@
 def per_device(perturb, pair_list, pair_count, band_weight, cov_scale, target, first_guess):
     w = gap_weights(pair_list, pair_count, band_weight, cov_scale)
     w_next = shifted(w, "space", -1)
-    p0 = lax.all_to_all(perturb, "space", split_axis=1, concat_axis=0, tiled=True)
+    p0 = rotated_exchange(perturb, "space", 1, 0)
     p1 = shifted(p0, "space", -1)
     p3 = shifted(p0, "space", -3)
     x0 = first_guess

time: 172 us -> 181 us (1.052)
  the two profiles are of different devices: /device:TPU:2 before, /device:TPU:4 now
where the time goes in v1:
time: 181 us
  waiting for transfers between devices  98.7 us (55%)
  starting transfers between devices  46.2 us (26%)
  between operations  15.5 us (9%)
  matrix products  15.4 us (9%)
  local copies, waits for them, and re-layouts  4.79 us (3%)
    ppermute x11, waiting for transfers between devices, shifted(): lax.ppermute(array, axis, [(i, (i + by) % count) for i in range(count)])  81.5 us
    ppermute x15, starting transfers between devices, rotated_exchange(): lax.ppermute(sent, axis, [(i, (i + lap) % length) for i in range(length)])  28.1 us
    ppermute x11, starting transfers between devices, shifted(): lax.ppermute(array, axis, [(i, (i + by) % count) for i in range(count)])  18.1 us
    psum x1, waiting for transfers between devices, per_device(): t0, t1, t2, t3 = lax.psum((t0, t1, t2, t3), 'mem')  15.4 us
    dot_general x18, matrix products, mm(): lax.dot_general(a, b, (((ca,), (cb,)), ((), ())), precision=lax.Precision...  15.4 us
  transfers between devices with their start and end apart: 27, of which 10 were waited for; matrix products, arithmetic and copies ran while one was open for 6% of the time, Pallas kernels for 0%

profile of v1, /device:TPU:4, one launch (start us, length us, event | category | flops | bytes accessed | tf_op | source)
XLA Modules:
  0.0 181.0 jit_solution(12974716263955950814)
XLA Ops:
  8.4 1.5 collective-permute-start
  10.0 1.5 collective-permute-start.1
  11.5 2.4 %collective-permute-start.2 = (f32[1,32,256]{2,1,0:T(8,128)S(1)}, f32[1,32,256]{2,1,0:T(8,128)S(1)}, u32[]{:S(2)}, u32[]{:S(2)}) collective-permute-start(f32[1,32,256]{2,1,0:T(8,128)S(1)} %bitcast.113), channel_id=1, source_target_pairs={{0,6},{2,8},{4,10},{6,12},{8,14},{10,16},{12,18},{14,20},{16,22},{... | collective-permute-start | bytes 98312 | tf_op jit(solution)/shard_map/ppermute | solution.py:31
  14.0 1.6 collective-permute-start.3
  18.1 2.6 %collective-permute-start.5 = (f32[1,32,256]{2,1,0:T(8,128)S(1)}, f32[1,32,256]{2,1,0:T(8,128)S(1)}, u32[]{:S(2)}, u32[]{:S(2)}) collective-permute-start(f32[1,32,256]{2,1,0:T(8,128)S(1)} %bitcast.125), channel_id=1, source_target_pairs={{0,12},{2,14},{4,16},{6,18},{8,20},{10,22},{12,24},{14,26},{16,28}... | collective-permute-start | bytes 98312 | tf_op jit(solution)/shard_map/ppermute | solution.py:31
  20.7 3.5 %collective-permute-start.6 = (f32[1,32,256]{2,1,0:T(8,128)S(1)}, f32[1,32,256]{2,1,0:T(8,128)S(1)}, u32[]{:S(2)}, u32[]{:S(2)}) collective-permute-start(f32[1,32,256]{2,1,0:T(8,128)S(1)} %bitcast.124), channel_id=1, source_target_pairs={{0,14},{2,16},{4,18},{6,20},{8,22},{10,24},{12,26},{14,28},{16,30}... | collective-permute-start | bytes 98312 | tf_op jit(solution)/shard_map/ppermute | solution.py:31
  26.4 2.2 %collective-permute-start.9 = (f32[1,32,256]{2,1,0:T(8,128)S(1)}, f32[1,32,256]{2,1,0:T(8,128)S(1)}, u32[]{:S(2)}, u32[]{:S(2)}) collective-permute-start(f32[1,32,256]{2,1,0:T(8,128)S(1)} %bitcast.121), channel_id=1, source_target_pairs={{0,20},{2,22},{4,24},{6,26},{8,28},{10,30},{12,0},{14,2},{16,4},{1... | collective-permute-start | bytes 98312 | tf_op jit(solution)/shard_map/ppermute | solution.py:31
  28.6 3.2 %collective-permute-start.10 = (f32[1,32,256]{2,1,0:T(8,128)S(1)}, f32[1,32,256]{2,1,0:T(8,128)S(1)}, u32[]{:S(2)}, u32[]{:S(2)}) collective-permute-start(f32[1,32,256]{2,1,0:T(8,128)S(1)} %bitcast.120), channel_id=1, source_target_pairs={{0,22},{2,24},{4,26},{6,28},{8,30},{10,0},{12,2},{14,4},{16,6},{18... | collective-permute-start | bytes 98312 | tf_op jit(solution)/shard_map/ppermute | solution.py:31
  31.8 2.0 %collective-permute-start.11 = (f32[1,32,256]{2,1,0:T(8,128)S(1)}, f32[1,32,256]{2,1,0:T(8,128)S(1)}, u32[]{:S(2)}, u32[]{:S(2)}) collective-permute-start(f32[1,32,256]{2,1,0:T(8,128)S(1)} %bitcast.119), channel_id=1, source_target_pairs={{0,24},{2,26},{4,28},{6,30},{8,0},{10,2},{12,4},{14,6},{16,8},{18,... | collective-permute-start | bytes 98312 | tf_op jit(solution)/shard_map/ppermute | solution.py:31
  33.9 1.3 collective-permute-start.13
  35.2 3.7 %collective-permute-start.14 = (f32[1,32,256]{2,1,0:T(8,128)S(1)}, f32[1,32,256]{2,1,0:T(8,128)S(1)}, u32[]{:S(2)}, u32[]{:S(2)}) collective-permute-start(f32[1,32,256]{2,1,0:T(8,128)S(1)} %bitcast.116), channel_id=1, source_target_pairs={{0,30},{2,0},{4,2},{6,4},{8,6},{10,8},{12,10},{14,12},{16,14},{18,... | collective-permute-start | bytes 98312 | tf_op jit(solution)/shard_map/ppermute | solution.py:31
  40.7 3.4 %collective-permute-start.15 = (f32[512,256]{1,0:T(8,128)S(1)}, f32[512,256]{1,0:T(8,128)S(1)}, u32[]{:S(2)}, u32[]{:S(2)}) collective-permute-start(f32[512,256]{1,0:T(8,128)S(1)} %bitcast.104), channel_id=1, source_target_pairs={{0,30},{2,0},{4,2},{6,4},{8,6},{10,8},{12,10},{14,12},{16,14},{18,... | collective-permute-start | bytes 1572872 | tf_op jit(solution)/shard_map/ppermute | solution.py:38
  44.2 2.4 %collective-permute-start.17 = (f32[512,256]{1,0:T(8,128)S(1)}, f32[512,256]{1,0:T(8,128)S(1)}, u32[]{:S(2)}, u32[]{:S(2)}) collective-permute-start(f32[512,256]{1,0:T(8,128)S(1)} %bitcast.105), channel_id=1, source_target_pairs={{0,26},{2,28},{4,30},{6,0},{8,2},{10,4},{12,6},{14,8},{16,10},{18,... | collective-permute-start | bytes 1572872 | tf_op jit(solution)/shard_map/ppermute | solution.py:38
  47.2 14.6 %collective-permute-done.19 = f32[4]{0:T(128)S(1)} collective-permute-done((f32[4]{0:T(128)S(1)}, f32[4]{0:T(128)S(1)}, u32[]{:S(2)}, u32[]{:S(2)}) %collective-permute-start.19) | collective-permute-done | bytes 48 | tf_op jit(solution)/shard_map/ppermute | solution.py:38
  62.4 1.9 %fusion.7 = f32[256,256]{1,0:T(8,128)} fusion(f32[16,32,256]{2,1,0:T(8,128)S(1)} %constant_dynamic-update-slice_fusion, f32[]{:T(128)} %bitcast.4), kind=kOutput, calls=%fused_computation.16 | convolution fusion | flops 201392128 | bytes 786436 | tf_op jit(solution)/shard_map/dot_general | solution.py:42
  64.3 1.9 %convolution_multiply_fusion.2 = f32[256,256]{1,0:T(8,128)} fusion(f32[512,256]{1,0:T(8,128)S(1)} %bitcast.106, f32[512,256]{1,0:T(8,128)S(1)} %collective-permute-done.15, f32[]{:T(128)} %bitcast.6), kind=kOutput, calls=%fused_computation.19 | convolution fusion | flops 201392128 | bytes 1310724 | tf_op jit(solution)/shard_map/dot_general | solution.py:42
  66.2 1.9 %convolution_multiply_fusion = f32[256,256]{1,0:T(8,128)} fusion(f32[512,256]{1,0:T(8,128)S(1)} %collective-permute-done.15, f32[512,256]{1,0:T(8,128)S(1)} %collective-permute-done.17, f32[]{:T(128)} %bitcast.8), kind=kOutput, calls=%fused_computation.17 | convolution fusion | flops 201392128 | bytes 1310724 | tf_op jit(solution)/shard_map/dot_general | solution.py:42
  68.0 2.0 %convolution_multiply_fusion.1 = f32[256,256]{1,0:T(8,128)} fusion(f32[512,256]{1,0:T(8,128)S(1)} %bitcast.107, f32[512,256]{1,0:T(8,128)S(1)} %collective-permute-done.17, f32[]{:T(128)} %bitcast.7), kind=kOutput, calls=%fused_computation.18 | convolution fusion | flops 201392128 | bytes 1310724 | tf_op jit(solution)/shard_map/dot_general | solution.py:42
  71.1 2.8 %collective-permute-start.18 = (f32[256,512]{1,0:T(8,128)S(1)}, f32[256,512]{1,0:T(8,128)S(1)}, u32[]{:S(2)}, u32[]{:S(2)}) collective-permute-start(f32[256,512]{1,0:T(8,128)S(1)} %copy-done), channel_id=1, source_target_pairs={{0,26},{2,28},{4,30},{6,0},{8,2},{10,4},{12,6},{14,8},{16,10},{18,... | collective-permute-start | bytes 1572872 | tf_op jit(solution)/shard_map/ppermute | solution.py:38
  74.5 15.4 %all-reduce.3.cloned.1.call-done = (f32[256,256]{1,0:T(8,128)}, f32[256,256]{1,0:T(8,128)}, f32[256,256]{1,0:T(8,128)}, f32[256,256]{1,0:T(8,128)}) async-done(((f32[256,256]{1,0:T(8,128)}, f32[256,256]{1,0:T(8,128)}, f32[256,256]{1,0:T(8,128)}, f32[256,256]{1,0:T(8,128)}), (f32[256,256]{1,0:T(8,128)}, f32[256,256]{1,0:T(8,128)}, f32[256,256]{1,0:T(8,128)}, ...) | async-done | bytes 1048592 | tf_op jit(solution)/shard_map/psum | solution.py:76
  89.9 1.4 fusion.13
  91.8 1.5 collective-permute-start.20
  94.2 2.4 %collective-permute-start.21 = (f32[256,512]{1,0:T(8,128)S(1)}, f32[256,512]{1,0:T(8,128)S(1)}, u32[]{:S(2)}, u32[]{:S(2)}) collective-permute-start(f32[256,512]{1,0:T(8,128)S(1)} %convolution_add_fusion.4), channel_id=1, source_target_pairs={{0,6},{2,8},{4,10},{6,12},{8,14},{10,16},{12,18},{14,20},{16,22},{... | collective-permute-start | bytes 1572872 | tf_op jit(solution)/shard_map/ppermute | solution.py:38
  98.0 20.2 %collective-permute-done.20 = f32[256,512]{1,0:T(8,128)S(1)} collective-permute-done((f32[256,512]{1,0:T(8,128)S(1)}, f32[256,512]{1,0:T(8,128)S(1)}, u32[]{:S(2)}, u32[]{:S(2)}) %collective-permute-start.20) | collective-permute-done | bytes 524320 | tf_op jit(solution)/shard_map/ppermute | solution.py:38
  118.1 1.5 collective-permute-done.21
  120.2 1.8 collective-permute-start.23
  122.0 2.4 %collective-permute-start.22 = (f32[256,512]{1,0:T(8,128)S(1)}, f32[256,512]{1,0:T(8,128)S(1)}, u32[]{:S(2)}, u32[]{:S(2)}) collective-permute-start(f32[256,512]{1,0:T(8,128)S(1)} %fusion.6), channel_id=1, source_target_pairs={{0,30},{2,0},{4,2},{6,4},{8,6},{10,8},{12,10},{14,12},{16,14},{18,... | collective-permute-start | bytes 1572872 | tf_op jit(solution)/shard_map/ppermute | solution.py:38
  124.3 11.2 %collective-permute-done.23 = f32[256,512]{1,0:T(8,128)S(1)} collective-permute-done((f32[256,512]{1,0:T(8,128)S(1)}, f32[256,512]{1,0:T(8,128)S(1)}, u32[]{:S(2)}, u32[]{:S(2)}) %collective-permute-start.23) | collective-permute-done | bytes 524320 | tf_op jit(solution)/shard_map/ppermute | solution.py:38
  137.1 18.9 %collective-permute-done.22 = f32[256,512]{1,0:T(8,128)S(1)} collective-permute-done((f32[256,512]{1,0:T(8,128)S(1)}, f32[256,512]{1,0:T(8,128)S(1)}, u32[]{:S(2)}, u32[]{:S(2)}) %collective-permute-start.22) | collective-permute-done | bytes 524320 | tf_op jit(solution)/shard_map/ppermute | solution.py:38
  157.7 11.4 %collective-permute-done.24 = f32[256,512]{1,0:T(8,128)S(1)} collective-permute-done((f32[256,512]{1,0:T(8,128)S(1)}, f32[256,512]{1,0:T(8,128)S(1)}, u32[]{:S(2)}, u32[]{:S(2)}) %collective-permute-start.24) | collective-permute-done | bytes 524320 | tf_op jit(solution)/shard_map/ppermute | solution.py:38
  169.1 3.8 %collective-permute-done.25 = f32[256,512]{1,0:T(8,128)S(1)} collective-permute-done((f32[256,512]{1,0:T(8,128)S(1)}, f32[256,512]{1,0:T(8,128)S(1)}, u32[]{:S(2)}, u32[]{:S(2)}) %collective-permute-start.25) | collective-permute-done | bytes 524320 | tf_op jit(solution)/shard_map/ppermute | solution.py:38
  172.9 1.3 multiply_add_fusion
  (98 shorter events, 16.0 us)
Async XLA Ops:
  6.5 83.4 %all-reduce.3.cloned.1.call-start = ((), (), s32[]{:S(2)}) async-start(), calls=%async_computation | async-start | bytes 2097152 | tf_op jit(solution)/shard_map/psum | solution.py:76
  7.8 8.0 %copy-start.7 = (s32[4,3]{1,0:T(4,128)S(1)}, s32[4,3]{1,0:T(4,128)}, u32[]{:S(2)}) copy-start(s32[4,3]{1,0:T(4,128)} %param.8) | copy-start | bytes 148
  7.8 8.2 %copy-start.8 = (f32[8]{0:T(128)S(1)}, f32[8]{0:T(128)}, u32[]{:S(2)}) copy-start(f32[8]{0:T(128)} %param.10) | copy-start | bytes 100
  8.4 8.1 %copy-start.5 = (f32[32,4096]{1,0:T(8,128)S(1)}, f32[32,4096]{1,0:T(8,128)}, u32[]{:S(2)}) copy-start(f32[32,4096]{1,0:T(8,128)} %param.7) | copy-start | bytes 1572868
  8.4 9.6 %collective-permute-start = (f32[1,32,256]{2,1,0:T(8,128)S(1)}, f32[1,32,256]{2,1,0:T(8,128)S(1)}, u32[]{:S(2)}, u32[]{:S(2)}) collective-permute-start(f32[1,32,256]{2,1,0:T(8,128)S(1)} %bitcast.115), channel_id=1, source_target_pairs={{0,2},{2,4},{4,6},{6,8},{8,10},{10,12},{12,14},{14,16},{16,18},{18... | collective-permute-start | bytes 98312 | tf_op jit(solution)/shard_map/ppermute | solution.py:31
  10.0 10.7 %collective-permute-start.1 = (f32[1,32,256]{2,1,0:T(8,128)S(1)}, f32[1,32,256]{2,1,0:T(8,128)S(1)}, u32[]{:S(2)}, u32[]{:S(2)}) collective-permute-start(f32[1,32,256]{2,1,0:T(8,128)S(1)} %bitcast.114), channel_id=1, source_target_pairs={{0,4},{2,6},{4,8},{6,10},{8,12},{10,14},{12,16},{14,18},{16,20},{1... | collective-permute-start | bytes 98312 | tf_op jit(solution)/shard_map/ppermute | solution.py:31
  11.5 12.7 %collective-permute-start.2 = (f32[1,32,256]{2,1,0:T(8,128)S(1)}, f32[1,32,256]{2,1,0:T(8,128)S(1)}, u32[]{:S(2)}, u32[]{:S(2)}) collective-permute-start(f32[1,32,256]{2,1,0:T(8,128)S(1)} %bitcast.113), channel_id=1, source_target_pairs={{0,6},{2,8},{4,10},{6,12},{8,14},{10,16},{12,18},{14,20},{16,22},{... | collective-permute-start | bytes 98312 | tf_op jit(solution)/shard_map/ppermute | solution.py:31
  14.0 11.5 %collective-permute-start.3 = (f32[1,32,256]{2,1,0:T(8,128)S(1)}, f32[1,32,256]{2,1,0:T(8,128)S(1)}, u32[]{:S(2)}, u32[]{:S(2)}) collective-permute-start(f32[1,32,256]{2,1,0:T(8,128)S(1)} %bitcast.112), channel_id=1, source_target_pairs={{0,8},{2,10},{4,12},{6,14},{8,16},{10,18},{12,20},{14,22},{16,24},... | collective-permute-start | bytes 98312 | tf_op jit(solution)/shard_map/ppermute | solution.py:31
  15.5 10.8 %collective-permute-start.4 = (f32[1,32,256]{2,1,0:T(8,128)S(1)}, f32[1,32,256]{2,1,0:T(8,128)S(1)}, u32[]{:S(2)}, u32[]{:S(2)}) collective-permute-start(f32[1,32,256]{2,1,0:T(8,128)S(1)} %bitcast.111), channel_id=1, source_target_pairs={{0,10},{2,12},{4,14},{6,16},{8,18},{10,20},{12,22},{14,24},{16,26}... | collective-permute-start | bytes 98312 | tf_op jit(solution)/shard_map/ppermute | solution.py:31
  18.1 10.5 %collective-permute-start.5 = (f32[1,32,256]{2,1,0:T(8,128)S(1)}, f32[1,32,256]{2,1,0:T(8,128)S(1)}, u32[]{:S(2)}, u32[]{:S(2)}) collective-permute-start(f32[1,32,256]{2,1,0:T(8,128)S(1)} %bitcast.125), channel_id=1, source_target_pairs={{0,12},{2,14},{4,16},{6,18},{8,20},{10,22},{12,24},{14,26},{16,28}... | collective-permute-start | bytes 98312 | tf_op jit(solution)/shard_map/ppermute | solution.py:31
  20.7 11.1 %collective-permute-start.6 = (f32[1,32,256]{2,1,0:T(8,128)S(1)}, f32[1,32,256]{2,1,0:T(8,128)S(1)}, u32[]{:S(2)}, u32[]{:S(2)}) collective-permute-start(f32[1,32,256]{2,1,0:T(8,128)S(1)} %bitcast.124), channel_id=1, source_target_pairs={{0,14},{2,16},{4,18},{6,20},{8,22},{10,24},{12,26},{14,28},{16,30}... | collective-permute-start | bytes 98312 | tf_op jit(solution)/shard_map/ppermute | solution.py:31
  24.2 9.6 %collective-permute-start.7 = (f32[1,32,256]{2,1,0:T(8,128)S(1)}, f32[1,32,256]{2,1,0:T(8,128)S(1)}, u32[]{:S(2)}, u32[]{:S(2)}) collective-permute-start(f32[1,32,256]{2,1,0:T(8,128)S(1)} %bitcast.123), channel_id=1, source_target_pairs={{0,16},{2,18},{4,20},{6,22},{8,24},{10,26},{12,28},{14,30},{16,0},... | collective-permute-start | bytes 98312 | tf_op jit(solution)/shard_map/ppermute | solution.py:31
  25.5 8.4 %collective-permute-start.8 = (f32[1,32,256]{2,1,0:T(8,128)S(1)}, f32[1,32,256]{2,1,0:T(8,128)S(1)}, u32[]{:S(2)}, u32[]{:S(2)}) collective-permute-start(f32[1,32,256]{2,1,0:T(8,128)S(1)} %bitcast.122), channel_id=1, source_target_pairs={{0,18},{2,20},{4,22},{6,24},{8,26},{10,28},{12,30},{14,0},{16,2},{... | collective-permute-start | bytes 98312 | tf_op jit(solution)/shard_map/ppermute | solution.py:31
  26.4 8.8 %collective-permute-start.9 = (f32[1,32,256]{2,1,0:T(8,128)S(1)}, f32[1,32,256]{2,1,0:T(8,128)S(1)}, u32[]{:S(2)}, u32[]{:S(2)}) collective-permute-start(f32[1,32,256]{2,1,0:T(8,128)S(1)} %bitcast.121), channel_id=1, source_target_pairs={{0,20},{2,22},{4,24},{6,26},{8,28},{10,30},{12,0},{14,2},{16,4},{1... | collective-permute-start | bytes 98312 | tf_op jit(solution)/shard_map/ppermute | solution.py:31
  28.6 10.3 %collective-permute-start.10 = (f32[1,32,256]{2,1,0:T(8,128)S(1)}, f32[1,32,256]{2,1,0:T(8,128)S(1)}, u32[]{:S(2)}, u32[]{:S(2)}) collective-permute-start(f32[1,32,256]{2,1,0:T(8,128)S(1)} %bitcast.120), channel_id=1, source_target_pairs={{0,22},{2,24},{4,26},{6,28},{8,30},{10,0},{12,2},{14,4},{16,6},{18... | collective-permute-start | bytes 98312 | tf_op jit(solution)/shard_map/ppermute | solution.py:31
  31.8 7.2 %collective-permute-start.11 = (f32[1,32,256]{2,1,0:T(8,128)S(1)}, f32[1,32,256]{2,1,0:T(8,128)S(1)}, u32[]{:S(2)}, u32[]{:S(2)}) collective-permute-start(f32[1,32,256]{2,1,0:T(8,128)S(1)} %bitcast.119), channel_id=1, source_target_pairs={{0,24},{2,26},{4,28},{6,30},{8,0},{10,2},{12,4},{14,6},{16,8},{18,... | collective-permute-start | bytes 98312 | tf_op jit(solution)/shard_map/ppermute | solution.py:31
  33.8 5.8 %collective-permute-start.12 = (f32[1,32,256]{2,1,0:T(8,128)S(1)}, f32[1,32,256]{2,1,0:T(8,128)S(1)}, u32[]{:S(2)}, u32[]{:S(2)}) collective-permute-start(f32[1,32,256]{2,1,0:T(8,128)S(1)} %bitcast.118), channel_id=1, source_target_pairs={{0,26},{2,28},{4,30},{6,0},{8,2},{10,4},{12,6},{14,8},{16,10},{18,... | collective-permute-start | bytes 98312 | tf_op jit(solution)/shard_map/ppermute | solution.py:31
  33.9 5.7 %collective-permute-start.13 = (f32[1,32,256]{2,1,0:T(8,128)S(1)}, f32[1,32,256]{2,1,0:T(8,128)S(1)}, u32[]{:S(2)}, u32[]{:S(2)}) collective-permute-start(f32[1,32,256]{2,1,0:T(8,128)S(1)} %bitcast.117), channel_id=1, source_target_pairs={{0,28},{2,30},{4,0},{6,2},{8,4},{10,6},{12,8},{14,10},{16,12},{18,... | collective-permute-start | bytes 98312 | tf_op jit(solution)/shard_map/ppermute | solution.py:31
  35.2 5.5 %collective-permute-start.14 = (f32[1,32,256]{2,1,0:T(8,128)S(1)}, f32[1,32,256]{2,1,0:T(8,128)S(1)}, u32[]{:S(2)}, u32[]{:S(2)}) collective-permute-start(f32[1,32,256]{2,1,0:T(8,128)S(1)} %bitcast.116), channel_id=1, source_target_pairs={{0,30},{2,0},{4,2},{6,4},{8,6},{10,8},{12,10},{14,12},{16,14},{18,... | collective-permute-start | bytes 98312 | tf_op jit(solution)/shard_map/ppermute | solution.py:31
  40.7 23.6 %collective-permute-start.15 = (f32[512,256]{1,0:T(8,128)S(1)}, f32[512,256]{1,0:T(8,128)S(1)}, u32[]{:S(2)}, u32[]{:S(2)}) collective-permute-start(f32[512,256]{1,0:T(8,128)S(1)} %bitcast.104), channel_id=1, source_target_pairs={{0,30},{2,0},{4,2},{6,4},{8,6},{10,8},{12,10},{14,12},{16,14},{18,... | collective-permute-start | bytes 1572872 | tf_op jit(solution)/shard_map/ppermute | solution.py:38
  44.2 17.6 %collective-permute-start.19 = (f32[4]{0:T(128)S(1)}, f32[4]{0:T(128)S(1)}, u32[]{:S(2)}, u32[]{:S(2)}) collective-permute-start(f32[4]{0:T(128)S(1)} %select_reduce_fusion), channel_id=1, source_target_pairs={{0,30},{2,0},{4,2},{6,4},{8,6},{10,8},{12,10},{14,12},{16,14},{18,... | collective-permute-start | bytes 56 | tf_op jit(solution)/shard_map/ppermute | solution.py:38
  44.2 22.0 %collective-permute-start.17 = (f32[512,256]{1,0:T(8,128)S(1)}, f32[512,256]{1,0:T(8,128)S(1)}, u32[]{:S(2)}, u32[]{:S(2)}) collective-permute-start(f32[512,256]{1,0:T(8,128)S(1)} %bitcast.105), channel_id=1, source_target_pairs={{0,26},{2,28},{4,30},{6,0},{8,2},{10,4},{12,6},{14,8},{16,10},{18,... | collective-permute-start | bytes 1572872 | tf_op jit(solution)/shard_map/ppermute | solution.py:38
  71.1 20.3 %collective-permute-start.18 = (f32[256,512]{1,0:T(8,128)S(1)}, f32[256,512]{1,0:T(8,128)S(1)}, u32[]{:S(2)}, u32[]{:S(2)}) collective-permute-start(f32[256,512]{1,0:T(8,128)S(1)} %copy-done), channel_id=1, source_target_pairs={{0,26},{2,28},{4,30},{6,0},{8,2},{10,4},{12,6},{14,8},{16,10},{18,... | collective-permute-start | bytes 1572872 | tf_op jit(solution)/shard_map/ppermute | solution.py:38
  73.9 19.9 %collective-permute-start.16 = (f32[256,512]{1,0:T(8,128)S(1)}, f32[256,512]{1,0:T(8,128)S(1)}, u32[]{:S(2)}, u32[]{:S(2)}) collective-permute-start(f32[256,512]{1,0:T(8,128)S(1)} %copy-done), channel_id=1, source_target_pairs={{0,30},{2,0},{4,2},{6,4},{8,6},{10,8},{12,10},{14,12},{16,14},{18,... | collective-permute-start | bytes 1572872 | tf_op jit(solution)/shard_map/ppermute | solution.py:38
  91.8 26.4 %collective-permute-start.20 = (f32[256,512]{1,0:T(8,128)S(1)}, f32[256,512]{1,0:T(8,128)S(1)}, u32[]{:S(2)}, u32[]{:S(2)}) collective-permute-start(f32[256,512]{1,0:T(8,128)S(1)} %convolution_add_fusion.5), channel_id=1, source_target_pairs={{0,2},{2,4},{4,6},{6,8},{8,10},{10,12},{12,14},{14,16},{16,18},{18... | collective-permute-start | bytes 1572872 | tf_op jit(solution)/shard_map/ppermute | solution.py:38
  93.7 2.9 %copy-start.6 = (f32[256,256]{1,0:T(8,128)S(1)}, f32[256,256]{1,0:T(8,128)}, u32[]{:S(2)}) copy-start(f32[256,256]{1,0:T(8,128)} %get-tuple-element.10) | copy-start | bytes 786436
  94.2 25.4 %collective-permute-start.21 = (f32[256,512]{1,0:T(8,128)S(1)}, f32[256,512]{1,0:T(8,128)S(1)}, u32[]{:S(2)}, u32[]{:S(2)}) collective-permute-start(f32[256,512]{1,0:T(8,128)S(1)} %convolution_add_fusion.4), channel_id=1, source_target_pairs={{0,6},{2,8},{4,10},{6,12},{8,14},{10,16},{12,18},{14,20},{16,22},{... | collective-permute-start | bytes 1572872 | tf_op jit(solution)/shard_map/ppermute | solution.py:38
  97.6 22.1 %copy-start.4 = (f32[256,512]{1,0:T(8,128)S(1)}, f32[256,512]{1,0:T(8,128)}, u32[]{:S(2)}) copy-start(f32[256,512]{1,0:T(8,128)} %param.12) | copy-start | bytes 1572868
  120.2 15.3 %collective-permute-start.23 = (f32[256,512]{1,0:T(8,128)S(1)}, f32[256,512]{1,0:T(8,128)S(1)}, u32[]{:S(2)}, u32[]{:S(2)}) collective-permute-start(f32[256,512]{1,0:T(8,128)S(1)} %fusion.6), channel_id=1, source_target_pairs={{0,26},{2,28},{4,30},{6,0},{8,2},{10,4},{12,6},{14,8},{16,10},{18,... | collective-permute-start | bytes 1572872 | tf_op jit(solution)/shard_map/ppermute | solution.py:38
  122.0 34.0 %collective-permute-start.22 = (f32[256,512]{1,0:T(8,128)S(1)}, f32[256,512]{1,0:T(8,128)S(1)}, u32[]{:S(2)}, u32[]{:S(2)}) collective-permute-start(f32[256,512]{1,0:T(8,128)S(1)} %fusion.6), channel_id=1, source_target_pairs={{0,30},{2,0},{4,2},{6,4},{8,6},{10,8},{12,10},{14,12},{16,14},{18,... | collective-permute-start | bytes 1572872 | tf_op jit(solution)/shard_map/ppermute | solution.py:38
  136.3 32.8 %collective-permute-start.24 = (f32[256,512]{1,0:T(8,128)S(1)}, f32[256,512]{1,0:T(8,128)S(1)}, u32[]{:S(2)}, u32[]{:S(2)}) collective-permute-start(f32[256,512]{1,0:T(8,128)S(1)} %convolution_add_fusion.1), channel_id=1, source_target_pairs={{0,2},{2,4},{4,6},{6,8},{8,10},{10,12},{12,14},{14,16},{16,18},{18... | collective-permute-start | bytes 1572872 | tf_op jit(solution)/shard_map/ppermute | solution.py:38
  156.8 16.1 %collective-permute-start.25 = (f32[256,512]{1,0:T(8,128)S(1)}, f32[256,512]{1,0:T(8,128)S(1)}, u32[]{:S(2)}, u32[]{:S(2)}) collective-permute-start(f32[256,512]{1,0:T(8,128)S(1)} %convolution_add_fusion), channel_id=1, source_target_pairs={{0,6},{2,8},{4,10},{6,12},{8,14},{10,16},{12,18},{14,20},{16,22},{... | collective-permute-start | bytes 1572872 | tf_op jit(solution)/shard_map/ppermute | solution.py:38
  (4 other events, 5.4 us)
Sparse Core Ops, SparseCore 0:
  70.2 19.6 all-reduce.2
